TPU v7x, 32 devices: a whole 2x2x4 slice. The times are simulated.
32 devices in a mesh: gx: 4 (over z), gy: 4 (over y, x), gz: 2 (over core).
Axes of the slice: x: 2, y: 2, z: 4, core: 2. Of those that a mesh axis runs over, the one named last changes fastest.
Arguments:
- volume: float32 [9, 16, 256, 512], P(None, 'gz', 'gx', 'gy'), may hold values from -6 to 6
- materials: float32 [3, 16, 256, 512], P(None, 'gz', 'gx', 'gy'), may hold values from 0.4 to 1.2
- water_height: float32 [128, 4096], P(('gx', 'gy', 'gz')), may hold values from 2 to 4
- water_flow: float32 [2, 128, 4096], P(None, ('gx', 'gy', 'gz')), may hold values from -3 to 3
- owner_of: int32 [128], replicated, may hold values from 0 to 31, as said below
- patch_tile: int32 [128], replicated, may hold values from 0 to 511, as said below
Outputs:
- volume_next: float32 [9, 16, 256, 512], P(None, 'gz', 'gx', 'gy')
- water_next: float32 [3, 128, 4096], P(None, ('gx', 'gy', 'gz'))
Inputs may be any that keep to these rules, and one draw needn't show every extreme that they name: `owner_of`: every device index owns exactly 4 patches, and the tiles of one owner's patches lie in the blocks of 4 different devices along gx and gy. `patch_tile`: all values are distinct; the block of each device along gx and gy holds the tiles of exactly 4 * (number of devices along gz) patches.
All inputs are finite; a program needn't handle non-finite values.
Results may differ from a plain program's by a relative error of at most 0.0001.
Values sent between devices are 32-bit elements; how exact they have to be, the bound alone decides.
A program may use at most 128 MiB of HBM per device.

v0:
```python
import functools

import jax
import jax.numpy as jnp
from jax import lax
from jax.experimental import pallas as pl
from jax.experimental.pallas import tpu as pltpu
from jax.sharding import PartitionSpec as P

PATCH_DEV = 4
PS = 16
REFINE = 4
FP = 64
LANES = 128
MESH = pl.DeviceIdType.MESH

wave_ratio = 0.075
flux_ratio = 0.05
uplift_rate = 1.0
gravity = 1.0


def log2(n):
    assert n & (n - 1) == 0
    return n.bit_length() - 1


def iota(shape, dim):
    return lax.broadcasted_iota(jnp.int32, shape, dim)


def exact_dot(a, b):
    return jnp.dot(a, b, precision=lax.Precision.HIGHEST, preferred_element_type=jnp.float32)


def pick_sum(mask, values):
    picked = jnp.where(mask, values.astype(jnp.float32), 0.0)
    return jnp.sum(picked, axis=1, keepdims=True).astype(jnp.int32)


def six_neighbours(ext, yl, yr, f, z, z_index, rows, row0, depth):
    lane = iota((rows, LANES), 1)
    at = f * depth + z
    top = row0 + 8
    mid = ext[f, z_index, top : top + rows, :]
    left = jnp.where(
        lane == 0,
        pltpu.roll(yl[row0 : row0 + rows, :], (LANES - at) & (LANES - 1), 1),
        pltpu.roll(mid, 1, 1),
    )
    right = jnp.where(
        lane == LANES - 1,
        pltpu.roll(yr[row0 : row0 + rows, :], LANES - 1 - at, 1),
        pltpu.roll(mid, LANES - 1, 1),
    )
    return (
        ext[f, z_index + 1, top : top + rows, :],
        ext[f, z_index - 1, top : top + rows, :],
        ext[f, z_index, top + 1 : top + 1 + rows, :],
        ext[f, z_index, top - 1 : top - 1 + rows, :],
        right,
        left,
    )


def mean_of(six):
    return (six[0] + six[1] + six[2] + six[3] + six[4] + six[5]) * (1.0 / 6.0)


def kernel(
    sizes,
    own_ref, til_ref, h_ref, fl_ref, vol_hbm, mat_hbm,
    vout_hbm, wout_ref,
    ext, mat, outv, ys_lo, ys_hi, yl, yr, strips, slots, lifts,
    vol_sem, mat_sem, out_sem, halo_send, halo_recv, st_send, st_recv, sib_send, sib_recv,
    lift_send, lift_recv,
):
    ngx, ngy, ngz, patches, depth, cx = sizes
    ndev = ngx * ngy * ngz
    nblk = ngx * ngy
    gx, gy, gz = lax.axis_index("gx"), lax.axis_index("gy"), lax.axis_index("gz")
    blk = gx * ngy + gy
    me = blk * ngz + gz
    local_x, local_y = cx // PS, LANES // PS
    tiles_x, tiles_y = local_x * ngx, local_y * ngy

    def coords(d):
        return (d // (ngy * ngz), (d // ngz) % ngy, d % ngz)

    vol_copy = pltpu.make_async_copy(
        vol_hbm, ext.at[:, pl.ds(1, depth), pl.ds(8, cx), :], vol_sem
    )
    vol_copy.start()
    mat_copy = pltpu.make_async_copy(mat_hbm, mat, mat_sem)
    mat_copy.start()

    barrier = pltpu.get_barrier_semaphore()

    def greet(i, carry):
        pl.semaphore_signal(
            barrier, inc=1, device_id=coords((me + i) % ndev), device_id_type=MESH
        )
        return carry

    lax.fori_loop(1, ndev, greet, 0)

    @pl.when(gz == 0)
    def _():
        ext[:, 0] = jnp.zeros_like(ext[:, 0])

    @pl.when(gz == ngz - 1)
    def _():
        ext[:, depth + 1] = jnp.zeros_like(ext[:, depth + 1])

    @pl.when(gx == 0)
    def _():
        ext[:, 1 : depth + 1, 7:8, :] = jnp.zeros((9, depth, 1, LANES), jnp.float32)

    @pl.when(gx == ngx - 1)
    def _():
        ext[:, 1 : depth + 1, cx + 8 : cx + 9, :] = jnp.zeros((9, depth, 1, LANES), jnp.float32)

    @pl.when(gy == 0)
    def _():
        yl[...] = jnp.zeros_like(yl)

    @pl.when(gy == ngy - 1)
    def _():
        yr[...] = jnp.zeros_like(yr)

    lane4 = iota((PATCH_DEV, LANES), 1)
    half = lane4 & (FP - 1)
    state = [h_ref[...], fl_ref[0], fl_ref[1]]
    groups = FP * FP // LANES
    for c in range(3):
        st = state[c]
        strips[gz, blk, 4 * c : 4 * c + 4, :] = jnp.where(
            lane4 < FP, st[:, :LANES], st[:, FP * FP - LANES :]
        )
        packed = jnp.zeros((PATCH_DEV, LANES), jnp.float32)
        for k in range(groups):
            part = st[:, LANES * k : LANES * (k + 1)]
            first = part if k == 0 else pltpu.roll(part, k, 1)
            packed = jnp.where(half == k, first, packed)
            packed = jnp.where(half == 32 + k, pltpu.roll(part, (k + 97) % LANES, 1), packed)
        strips[gz, blk, 12 + 4 * c : 16 + 4 * c, :] = packed

    vol_copy.wait()

    lane_c = iota((cx, LANES), 1)

    def pack(z, carry):
        lo, hi = carry
        for f in range(9):
            at = f * depth + z
            u = ext[f, z + 1, 8 : 8 + cx, :]
            lo = jnp.where(lane_c == at, pltpu.roll(u, at, 1), lo)
            hi = jnp.where(lane_c == at, pltpu.roll(u, at + 1, 1), hi)
        return lo, hi

    zero_face = jnp.zeros((cx, LANES), jnp.float32)
    lo, hi = lax.fori_loop(0, depth, pack, (zero_face, zero_face))
    ys_lo[...] = lo
    ys_hi[...] = hi

    pl.semaphore_wait(barrier, ndev - 1)

    def remote(src, dst, k, target):
        return pltpu.make_async_remote_copy(
            src_ref=src, dst_ref=dst, send_sem=halo_send.at[k], recv_sem=halo_recv.at[k],
            device_id=target, device_id_type=MESH,
        )

    inner = pl.ds(1, depth)
    halos = [
        (gy < ngy - 1, gy > 0, remote(ys_hi, yl, 0, (gx, gy + 1, gz))),
        (gy > 0, gy < ngy - 1, remote(ys_lo, yr, 1, (gx, gy - 1, gz))),
        (gx < ngx - 1, gx > 0, remote(
            ext.at[:, inner, pl.ds(cx + 7, 1), :], ext.at[:, inner, pl.ds(7, 1), :],
            2, (gx + 1, gy, gz))),
        (gx > 0, gx < ngx - 1, remote(
            ext.at[:, inner, pl.ds(8, 1), :], ext.at[:, inner, pl.ds(cx + 8, 1), :],
            3, (gx - 1, gy, gz))),
        (gz < ngz - 1, gz > 0, remote(
            ext.at[:, depth, pl.ds(8, cx), :], ext.at[:, 0, pl.ds(8, cx), :],
            4, (gx, gy, gz + 1))),
        (gz > 0, gz < ngz - 1, remote(
            ext.at[:, 1, pl.ds(8, cx), :], ext.at[:, depth + 1, pl.ds(8, cx), :],
            5, (gx, gy, gz - 1))),
    ]
    for has_target, _, copy in halos:
        pl.when(has_target)(copy.start)

    def spread(i, carry):
        b = (blk + i) % nblk
        pltpu.make_async_remote_copy(
            src_ref=strips.at[gz, blk], dst_ref=strips.at[gz, blk],
            send_sem=st_send, recv_sem=st_recv,
            device_id=(b // ngy, b % ngy, gz), device_id_type=MESH,
        ).start()
        return carry

    lax.fori_loop(1, nblk, spread, 0)

    owner = own_ref[...]
    tile = til_ref[...]
    square = (patches, patches)
    owner_wide = jnp.broadcast_to(owner, square)
    owner_col = pick_sum(iota(square, 0) == iota(square, 1), owner_wide)
    earlier = (owner_col == owner_wide) & (iota(square, 0) < iota(square, 1))
    rank = jnp.sum(jnp.where(earlier, 1.0, 0.0), axis=0, keepdims=True).astype(jnp.int32)
    row_of = owner * PATCH_DEV + rank
    tile_x = tile >> log2(tiles_y)
    tile_y = tile & (tiles_y - 1)
    wide8 = (8, patches)
    row_of8 = jnp.broadcast_to(row_of, wide8)
    tile8 = jnp.broadcast_to(tile, wide8)
    mine = row_of8 == me * PATCH_DEV + iota(wide8, 0)
    mine = mine & (iota(wide8, 0) < PATCH_DEV)
    my_tile = pick_sum(mine, tile8)
    my_x = my_tile >> log2(tiles_y)
    my_y = my_tile & (tiles_y - 1)
    my_blk = (my_x >> log2(local_x)) * ngy + (my_y >> log2(local_y))

    founds = []
    picks = []
    keys = (8, ndev * 24)
    for side, (valid, want) in enumerate(
        [
            (my_x > 0, my_tile - tiles_y),
            (my_x < tiles_x - 1, my_tile + tiles_y),
            (my_y > 0, my_tile - 1),
            (my_y < tiles_y - 1, my_tile + 1),
        ]
    ):
        match = tile8 == jnp.where(valid, want, -1)
        other = pick_sum(match, row_of8 + 1) - 1
        founds.append((other >= 0)[:PATCH_DEV])
        dev = other >> log2(PATCH_DEV)
        place = (dev & (ngz - 1)) * nblk + (dev >> log2(ngz))
        target = place * 24 + (other & (PATCH_DEV - 1))
        for c in range(3):
            q = c if side < 2 else 3 + c
            goal = jnp.where(other >= 0, target + 4 * q, -1)
            picks.append(jnp.where(iota(keys, 1) == goal, 1.0, 0.0))
    pick_all = jnp.concatenate(picks, axis=0)

    for k in range(4):
        pl.when(halos[k][1])(halos[k][2].wait_recv)
    mat_copy.wait()

    @pl.when(gz == 0)
    def _():
        def diff(f, along):
            six = six_neighbours(ext, yl, yr, f, 0, 1, cx, 0, depth)
            return six[2 * along] - six[2 * along + 1]

        def vz_sum():
            six = six_neighbours(ext, yl, yr, 2, 0, 1, cx, 0, depth)
            return mean_of(six)

        rate = mat[0, 0] * (diff(7, 1) + diff(8, 2) + diff(5, 0))
        floor = vz_sum() + wave_ratio * rate

        tall = (ndev * PS, patches)
        here = (
            (tile_x >> log2(local_x) == gx) & (tile_y >> log2(local_y) == gy)
        )
        owner_here = jnp.where(here, owner, -1)
        chosen = jnp.broadcast_to(owner_here, tall) == (iota(tall, 0) >> log2(PS))
        local = (tile_x & (local_x - 1)) * local_y + (tile_y & (local_y - 1)) + 1
        local_col = pick_sum(chosen, jnp.broadcast_to(local, tall)) - 1
        local_tx = local_col >> log2(local_y)
        local_ty = local_col & (local_y - 1)
        wide = (ndev * PS, cx)
        row_want = local_tx * PS + (iota((ndev * PS, 1), 0) & (PS - 1))
        band = exact_dot(jnp.where(iota(wide, 1) == row_want, 1.0, 0.0), floor)
        full = (ndev * PS, LANES)
        band = jnp.where((iota(full, 1) >> log2(PS)) == local_ty, band, 0.0)
        same = (iota((LANES, LANES), 0) & (PS - 1)) == (iota((LANES, LANES), 1) & (PS - 1))
        spread_lanes = exact_dot(band, jnp.where(same, 1.0, 0.0))
        kept = jnp.where(
            (iota(full, 1) >> log2(PS)) == (iota(full, 0) & 7), spread_lanes, 0.0
        )
        rows = jnp.sum(kept.reshape(ndev * 2, 8, LANES), axis=1)
        for d in range(ndev):
            slots[d] = rows[2 * d : 2 * d + 2, :]

        def send_lift(i, carry):
            d = (me + i) % ndev
            pltpu.make_async_remote_copy(
                src_ref=slots.at[d], dst_ref=lifts.at[blk],
                send_sem=lift_send, recv_sem=lift_recv,
                device_id=coords(d), device_id_type=MESH,
            ).start()
            return carry

        lax.fori_loop(1, ndev, send_lift, 0)
        lifts[blk] = slots[me]

    for k in range(4, 6):
        pl.when(halos[k][1])(halos[k][2].wait_recv)

    def layer(z, carry):
        for row0 in range(0, cx, 16):
            sixes = {}

            def six(f):
                if f not in sixes:
                    sixes[f] = six_neighbours(ext, yl, yr, f, z, z + 1, 16, row0, depth)
                return sixes[f]

            def across(f, along):
                return six(f)[2 * along] - six(f)[2 * along + 1]

            def put(f, rate):
                outv[f, z, row0 : row0 + 16, :] = mean_of(six(f)) + wave_ratio * rate

            buoyancy = mat[0, z, row0 : row0 + 16, :]
            lame = mat[1, z, row0 : row0 + 16, :]
            shear = mat[2, z, row0 : row0 + 16, :]
            dx, dy, dz = across(0, 1), across(1, 2), across(2, 0)
            ldiv = lame * (dx + dy + dz)
            put(0, buoyancy * (across(3, 1) + across(6, 2) + across(7, 0)))
            put(1, buoyancy * (across(6, 1) + across(4, 2) + across(8, 0)))
            put(2, buoyancy * (across(7, 1) + across(8, 2) + across(5, 0)))
            put(3, ldiv + 2.0 * shear * dx)
            put(4, ldiv + 2.0 * shear * dy)
            put(5, ldiv + 2.0 * shear * dz)
            put(6, shear * (across(0, 2) + across(1, 1)))
            put(7, shear * (across(0, 0) + across(2, 1)))
            put(8, shear * (across(1, 0) + across(2, 2)))
        return carry

    def store_layers(start, count, k):
        return pltpu.make_async_copy(
            outv.at[:, pl.ds(start, count)], vout_hbm.at[:, pl.ds(start, count)], out_sem.at[k]
        )

    first_part = depth // 2
    lax.fori_loop(0, first_part, layer, 0)
    store_a = store_layers(0, first_part, 0)
    store_a.start()

    some = strips.at[gz, pl.ds(0, nblk - 1)]
    pltpu.make_async_copy(some, some, st_recv).wait()

    def hand(i):
        other = (gz + i) % ngz
        return pltpu.make_async_remote_copy(
            src_ref=strips.at[gz], dst_ref=strips.at[gz],
            send_sem=sib_send.at[i - 1], recv_sem=sib_recv.at[i - 1],
            device_id=(gx, gy, other), device_id_type=MESH,
        )

    for i in range(1, ngz):
        hand(i).start()
    lax.fori_loop(first_part, depth, layer, 0)
    store_b = store_layers(first_part, depth - first_part, 1)
    store_b.start()

    for i in range(1, ngz):
        hand(i).wait_recv()
    ghosts = exact_dot(pick_all, strips[...].reshape(ndev * 24, LANES))

    @pl.when(gz == 0)
    def _():
        part = lifts.at[pl.ds(0, nblk - 1)]
        pltpu.make_async_copy(part, part, lift_recv).wait()

    @pl.when(gz != 0)
    def _():
        pltpu.make_async_copy(lifts, lifts, lift_recv).wait()

    chooser = jnp.where(iota((8, nblk), 1) == my_blk, 1.0, 0.0)
    coarse = [exact_dot(chooser, lifts[:, k, :]) for k in range(2)]
    wide_lane = iota((LANES, 8 * LANES), 1)
    source = (wide_lane >> log2(LANES)) * PS + ((wide_lane & (FP - 1)) >> log2(REFINE))
    expand = jnp.where(iota((LANES, 8 * LANES), 0) == source, 1.0, 0.0)
    fine = [exact_dot(coarse[k], expand)[:PATCH_DEV] for k in range(2)]
    lift = jnp.concatenate(
        [
            fine[(k // 2) // 8][:, LANES * ((k // 2) % 8) : LANES * ((k // 2) % 8 + 1)]
            for k in range(groups)
        ],
        axis=1,
    )

    lane = iota((PATCH_DEV, FP * FP), 1)
    col = lane & (FP - 1)

    def ghost(side, c):
        at = (side * 3 + c) * 8
        return ghosts[at : at + PATCH_DEV, :]

    def beside(c, side):
        st = state[c]
        g = ghost(side, c)
        if side == 0:
            wide = jnp.concatenate([pltpu.roll(g, FP, 1)] * groups, axis=1)
            edge, moved = lane < FP, pltpu.roll(st, FP, 1)
        elif side == 1:
            wide = jnp.concatenate([pltpu.roll(g, FP, 1)] * groups, axis=1)
            edge, moved = lane >= FP * FP - FP, pltpu.roll(st, FP * FP - FP, 1)
        elif side == 2:
            wide = jnp.concatenate([pltpu.roll(g, 96 - k, 1) for k in range(groups)], axis=1)
            edge, moved = col == 0, pltpu.roll(st, 1, 1)
        else:
            wide = jnp.concatenate([pltpu.roll(g, 63 - k, 1) for k in range(groups)], axis=1)
            edge, moved = col == FP - 1, pltpu.roll(st, FP * FP - 1, 1)
        return jnp.where(edge, jnp.where(founds[side], wide, st), moved)

    sides = [[beside(c, side) for c in range(3)] for side in range(4)]

    def fluxes_x(part):
        height, flow_x, flow_y = part
        speed = flow_x / height
        return [flow_x, flow_x * speed + 0.5 * gravity * height * height, flow_y * speed]

    def fluxes_y(part):
        height, flow_x, flow_y = part
        speed = flow_y / height
        return [flow_y, flow_x * speed, flow_y * speed + 0.5 * gravity * height * height]

    fw, fe = fluxes_x(sides[0]), fluxes_x(sides[1])
    fs, fn = fluxes_y(sides[2]), fluxes_y(sides[3])
    for c in range(3):
        updated = 0.25 * (sides[1][c] + sides[0][c] + sides[3][c] + sides[2][c]) - flux_ratio * (
            (fe[c] - fw[c]) + (fn[c] - fs[c])
        )
        if c == 0:
            updated = updated + uplift_rate * lift
        wout_ref[c] = updated

    store_a.wait()
    store_b.wait()
    for has_target, _, copy in halos:
        pl.when(has_target)(copy.wait_send)
    pltpu.make_async_copy(some, some, st_send).wait()
    for i in range(1, ngz):
        hand(i).wait_send()

    @pl.when(gz == 0)
    def _():
        sent = slots.at[pl.ds(0, ndev - 1)]
        pltpu.make_async_copy(sent, sent, lift_send).wait()


def per_device(volume, materials, water_height, water_flow, owner_of, patch_tile):
    ngx, ngy, ngz = (lax.axis_size(a) for a in ("gx", "gy", "gz"))
    ndev, nblk = ngx * ngy * ngz, ngx * ngy
    fields, depth, cx, cy = volume.shape
    patches = owner_of.shape[0]
    assert cy == LANES and fields * depth <= LANES
    f32 = jnp.float32
    dma = pltpu.SemaphoreType.DMA
    vmem = pl.BlockSpec(memory_space=pltpu.VMEM)
    anywhere = pl.BlockSpec(memory_space=pl.ANY)
    return pl.pallas_call(
        functools.partial(kernel, (ngx, ngy, ngz, patches, depth, cx)),
        name="coupled_step",
        out_shape=(
            jax.ShapeDtypeStruct(volume.shape, f32),
            jax.ShapeDtypeStruct((3,) + water_height.shape, f32),
        ),
        in_specs=[vmem, vmem, vmem, vmem, anywhere, anywhere],
        out_specs=(anywhere, vmem),
        scratch_shapes=[
            pltpu.VMEM((fields, depth + 2, cx + 16, LANES), f32),
            pltpu.VMEM(materials.shape, f32),
            pltpu.VMEM(volume.shape, f32),
            pltpu.VMEM((cx, LANES), f32),
            pltpu.VMEM((cx, LANES), f32),
            pltpu.VMEM((cx, LANES), f32),
            pltpu.VMEM((cx, LANES), f32),
            pltpu.VMEM((ngz, nblk, 24, LANES), f32),
            pltpu.VMEM((ndev, 2, LANES), f32),
            pltpu.VMEM((nblk, 2, LANES), f32),
            dma, dma, dma((2,)), dma((6,)), dma((6,)), dma, dma,
            dma((max(ngz - 1, 1),)), dma((max(ngz - 1, 1),)), dma, dma,
        ],
        compiler_params=pltpu.CompilerParams(collective_id=0, has_side_effects=True, vmem_limit_bytes=56 * 1024 * 1024),
    )(
        owner_of.reshape(1, patches), patch_tile.reshape(1, patches),
        water_height, water_flow, volume, materials,
    )


def solution(mesh):
    return jax.shard_map(
        per_device,
        mesh=mesh,
        in_specs=(
            P(None, "gz", "gx", "gy"),
            P(None, "gz", "gx", "gy"),
            P(("gx", "gy", "gz"), None),
            P(None, ("gx", "gy", "gz"), None),
            P(),
            P(),
        ),
        out_specs=(P(None, "gz", "gx", "gy"), P(None, ("gx", "gy", "gz"), None)),
        check_vma=False,
    )
```

profile of v0, /device:TPU:0, one launch (start us, length us, event | category | flops | bytes accessed | tf_op | source)
XLA Modules:
  0.0 24.4 jit_solution(9313386144727319163)
XLA Ops:
  0.6 19.7 %coupled_step.1 = (f32[9,8,64,128]{3,2,1,0:T(8,128)}, f32[3,4,4096]{2,1,0:T(4,128)}) custom-call(s32[1,128]{1,0:T(1,128)} %bitcast.2, s32[1,128]{1,0:T(1,128)} %bitcast.3, f32[4,4096]{1,0:T(4,128)} %h_ref.1, f32[2,4,4096]{2,1,0:T(4,128)} %fl_ref.1, f32[9,8,64,128]{3,2,1,0:T(8,128)} %vol_hbm.1, f32[3,8,64,128]{3,2,1,0:T(8,128)} %mat_hbm.1), custom_call_target="tpu_custom_call" | custom-call | tf_op jit(solution)/shard_map/coupled_step/pallas_call | solution.py:459
  20.3 0.0 copy-start
  20.3 3.4 %copy.10 = f32[9,8,64,128]{3,2,1,0:T(8,128)} copy(f32[9,8,64,128]{3,2,1,0:T(8,128)} %get-tuple-element.4) | data formatting | bytes 4718592
  23.7 0.0 copy-done
  23.7 0.7 %copy.11 = f32[3,4,4096]{2,1,0:T(4,128)} copy(f32[3,4,4096]{2,1,0:T(4,128)S(1)} %copy-done) | data formatting | bytes 393216
Async XLA Ops:
  20.3 3.4 %copy-start = (f32[3,4,4096]{2,1,0:T(4,128)S(1)}, f32[3,4,4096]{2,1,0:T(4,128)}, u32[]{:S(2)}) copy-start(f32[3,4,4096]{2,1,0:T(4,128)} %get-tuple-element.5) | copy-start | bytes 589828
where the time goes:
time: 24.6 us; the launch traced here: 24.4 us
  Pallas kernels  19.7 us (80%)
  local copies, waits for them, and re-layouts  4.08 us (17%)
  between operations  0.65 us (3%)
    pallas_call x1, Pallas kernels, per_device(): pl.pallas_call(functools.partial(kernel, (ngx, ngy, ngz, patches, depth,...  19.7 us
    unnamed x4, local copies, waits for them, and re-layouts  4.08 us

commit v1 on v0

--- a/solution.py
+++ b/solution.py
@@ -69,10 +69,10 @@
 
 def kernel(
     sizes,
-    own_ref, til_ref, h_ref, fl_ref, vol_hbm, mat_hbm,
-    vout_hbm, wout_ref,
-    ext, mat, outv, ys_lo, ys_hi, yl, yr, strips, slots, lifts,
-    vol_sem, mat_sem, out_sem, halo_send, halo_recv, st_send, st_recv, sib_send, sib_recv,
+    own_hbm, til_hbm, h_hbm, fl_hbm, vol_hbm, mat_hbm,
+    outv, state_out, ghosts_out, found_out, coarse_out,
+    ext, mat, ys_lo, ys_hi, yl, yr, strips, slots, lifts,
+    own_ref, til_ref, vol_sem, mat_sem, in_sem, halo_send, halo_recv, st_send, st_recv, sib_send, sib_recv,
     lift_send, lift_recv,
 ):
     ngx, ngy, ngz, patches, depth, cx = sizes
@@ -90,6 +90,14 @@
     vol_copy = pltpu.make_async_copy(
         vol_hbm, ext.at[:, pl.ds(1, depth), pl.ds(8, cx), :], vol_sem
     )
+    ins = [
+        pltpu.make_async_copy(h_hbm, state_out.at[0], in_sem.at[0]),
+        pltpu.make_async_copy(fl_hbm, state_out.at[pl.ds(1, 2)], in_sem.at[1]),
+        pltpu.make_async_copy(own_hbm, own_ref, in_sem.at[2]),
+        pltpu.make_async_copy(til_hbm, til_ref, in_sem.at[3]),
+    ]
+    for copy in ins:
+        copy.start()
     vol_copy.start()
     mat_copy = pltpu.make_async_copy(mat_hbm, mat, mat_sem)
     mat_copy.start()
@@ -130,7 +138,9 @@
 
     lane4 = iota((PATCH_DEV, LANES), 1)
     half = lane4 & (FP - 1)
-    state = [h_ref[...], fl_ref[0], fl_ref[1]]
+    for copy in ins:
+        copy.wait()
+    state = [state_out[0], state_out[1], state_out[2]]
     groups = FP * FP // LANES
     for c in range(3):
         st = state[c]
@@ -222,7 +232,6 @@
     my_y = my_tile & (tiles_y - 1)
     my_blk = (my_x >> log2(local_x)) * ngy + (my_y >> log2(local_y))
 
-    founds = []
     picks = []
     keys = (8, ndev * 24)
     for side, (valid, want) in enumerate(
@@ -235,7 +244,7 @@
     ):
         match = tile8 == jnp.where(valid, want, -1)
         other = pick_sum(match, row_of8 + 1) - 1
-        founds.append((other >= 0)[:PATCH_DEV])
+        found_out[side] = jnp.broadcast_to(jnp.where(other >= 0, 1.0, 0.0), (8, LANES))
         dev = other >> log2(PATCH_DEV)
         place = (dev & (ngz - 1)) * nblk + (dev >> log2(ngz))
         target = place * 24 + (other & (PATCH_DEV - 1))
@@ -245,44 +254,52 @@
             picks.append(jnp.where(iota(keys, 1) == goal, 1.0, 0.0))
     pick_all = jnp.concatenate(picks, axis=0)
 
+    chooser = jnp.where(iota((8, nblk), 1) == my_blk, 1.0, 0.0)
+    here = (tile_x >> log2(local_x) == gx) & (tile_y >> log2(local_y) == gy)
+    here_wide = jnp.broadcast_to(jnp.where(here, 1, 0), square)
+    here_col = pick_sum(iota(square, 0) == iota(square, 1), here_wide)
+    before = (here_col == 1) & (iota(square, 0) < iota(square, 1))
+    place_row = jnp.sum(jnp.where(before, 1.0, 0.0), axis=0, keepdims=True).astype(jnp.int32)
+    place_row = jnp.where(here, place_row, -1)
+    count = PATCH_DEV * ngz
+    tall = (count * PS, patches)
+    chosen = jnp.broadcast_to(place_row, tall) == (iota(tall, 0) >> log2(PS))
+    local = (tile_x & (local_x - 1)) * local_y + (tile_y & (local_y - 1)) + 1
+    local_col = pick_sum(chosen, jnp.broadcast_to(local, tall)) - 1
+    local_tx = local_col >> log2(local_y)
+    local_ty = local_col & (local_y - 1)
+    row_want = local_tx * PS + (iota((count * PS, 1), 0) & (PS - 1))
+    row_pick = jnp.where(iota((count * PS, cx), 1) == row_want, 1.0, 0.0)
+    full = (count * PS, LANES)
+    lane_pick = (iota(full, 1) >> log2(PS)) == local_ty
+    owner_here = jnp.where(here, owner, -1)
+    slot_wide = (2 * ndev, patches)
+    owned = jnp.broadcast_to(owner_here, slot_wide) == (iota(slot_wide, 0) >> 1)
+    slot_place = pick_sum(owned, jnp.broadcast_to(place_row + 1, slot_wide)) - 1
+    slot_row = jnp.where(slot_place >= 0, 2 * slot_place + (iota((2 * ndev, 1), 0) & 1), -1)
+    slot_pick = jnp.where(iota((2 * ndev, 2 * count), 1) == slot_row, 1.0, 0.0)
+
     for k in range(4):
         pl.when(halos[k][1])(halos[k][2].wait_recv)
     mat_copy.wait()
 
     @pl.when(gz == 0)
     def _():
-        def diff(f, along):
-            six = six_neighbours(ext, yl, yr, f, 0, 1, cx, 0, depth)
-            return six[2 * along] - six[2 * along + 1]
-
-        def vz_sum():
-            six = six_neighbours(ext, yl, yr, 2, 0, 1, cx, 0, depth)
-            return mean_of(six)
-
-        rate = mat[0, 0] * (diff(7, 1) + diff(8, 2) + diff(5, 0))
-        floor = vz_sum() + wave_ratio * rate
-
-        tall = (ndev * PS, patches)
-        here = (
-            (tile_x >> log2(local_x) == gx) & (tile_y >> log2(local_y) == gy)
-        )
-        owner_here = jnp.where(here, owner, -1)
-        chosen = jnp.broadcast_to(owner_here, tall) == (iota(tall, 0) >> log2(PS))
-        local = (tile_x & (local_x - 1)) * local_y + (tile_y & (local_y - 1)) + 1
-        local_col = pick_sum(chosen, jnp.broadcast_to(local, tall)) - 1
-        local_tx = local_col >> log2(local_y)
-        local_ty = local_col & (local_y - 1)
-        wide = (ndev * PS, cx)
-        row_want = local_tx * PS + (iota((ndev * PS, 1), 0) & (PS - 1))
-        band = exact_dot(jnp.where(iota(wide, 1) == row_want, 1.0, 0.0), floor)
-        full = (ndev * PS, LANES)
-        band = jnp.where((iota(full, 1) >> log2(PS)) == local_ty, band, 0.0)
+        def six(f):
+            return six_neighbours(ext, yl, yr, f, 0, 1, cx, 0, depth)
+
+        vz = six(2)
+        sxz, syz = six(7), six(8)
+        szz = ext[5, 2, 8 : 8 + cx, :] - ext[5, 0, 8 : 8 + cx, :]
+        rate = mat[0, 0] * ((sxz[2] - sxz[3]) + (syz[4] - syz[5]) + szz)
+        floor = mean_of(vz) + wave_ratio * rate
+        band = jnp.where(lane_pick, exact_dot(row_pick, floor), 0.0)
         same = (iota((LANES, LANES), 0) & (PS - 1)) == (iota((LANES, LANES), 1) & (PS - 1))
         spread_lanes = exact_dot(band, jnp.where(same, 1.0, 0.0))
         kept = jnp.where(
             (iota(full, 1) >> log2(PS)) == (iota(full, 0) & 7), spread_lanes, 0.0
         )
-        rows = jnp.sum(kept.reshape(ndev * 2, 8, LANES), axis=1)
+        rows = exact_dot(slot_pick, jnp.sum(kept.reshape(count * 2, 8, LANES), axis=1))
         for d in range(ndev):
             slots[d] = rows[2 * d : 2 * d + 2, :]
 
@@ -332,15 +349,8 @@
             put(8, shear * (across(1, 0) + across(2, 2)))
         return carry
 
-    def store_layers(start, count, k):
-        return pltpu.make_async_copy(
-            outv.at[:, pl.ds(start, count)], vout_hbm.at[:, pl.ds(start, count)], out_sem.at[k]
-        )
-
     first_part = depth // 2
     lax.fori_loop(0, first_part, layer, 0)
-    store_a = store_layers(0, first_part, 0)
-    store_a.start()
 
     some = strips.at[gz, pl.ds(0, nblk - 1)]
     pltpu.make_async_copy(some, some, st_recv).wait()
@@ -356,12 +366,10 @@
     for i in range(1, ngz):
         hand(i).start()
     lax.fori_loop(first_part, depth, layer, 0)
-    store_b = store_layers(first_part, depth - first_part, 1)
-    store_b.start()
 
     for i in range(1, ngz):
         hand(i).wait_recv()
-    ghosts = exact_dot(pick_all, strips[...].reshape(ndev * 24, LANES))
+    ghosts_out[...] = exact_dot(pick_all, strips[...].reshape(ndev * 24, LANES))
 
     @pl.when(gz == 0)
     def _():
@@ -372,12 +380,32 @@
     def _():
         pltpu.make_async_copy(lifts, lifts, lift_recv).wait()
 
-    chooser = jnp.where(iota((8, nblk), 1) == my_blk, 1.0, 0.0)
-    coarse = [exact_dot(chooser, lifts[:, k, :]) for k in range(2)]
+    for k in range(2):
+        coarse_out[k] = exact_dot(chooser, lifts[:, k, :])
+
+    for has_target, _, copy in halos:
+        pl.when(has_target)(copy.wait_send)
+    pltpu.make_async_copy(some, some, st_send).wait()
+    for i in range(1, ngz):
+        hand(i).wait_send()
+
+    @pl.when(gz == 0)
+    def _():
+        sent = slots.at[pl.ds(0, ndev - 1)]
+        pltpu.make_async_copy(sent, sent, lift_send).wait()
+
+
+def finish(
+    outv, state_ref, ghosts_ref, found_ref, coarse_ref, vout_hbm, wout_ref, out_sem
+):
+    store = pltpu.make_async_copy(outv, vout_hbm, out_sem)
+    store.start()
+    state = [state_ref[0], state_ref[1], state_ref[2]]
+    groups = FP * FP // LANES
     wide_lane = iota((LANES, 8 * LANES), 1)
     source = (wide_lane >> log2(LANES)) * PS + ((wide_lane & (FP - 1)) >> log2(REFINE))
     expand = jnp.where(iota((LANES, 8 * LANES), 0) == source, 1.0, 0.0)
-    fine = [exact_dot(coarse[k], expand)[:PATCH_DEV] for k in range(2)]
+    fine = [exact_dot(coarse_ref[k], expand)[:PATCH_DEV] for k in range(2)]
     lift = jnp.concatenate(
         [
             fine[(k // 2) // 8][:, LANES * ((k // 2) % 8) : LANES * ((k // 2) % 8 + 1)]
@@ -391,11 +419,12 @@
 
     def ghost(side, c):
         at = (side * 3 + c) * 8
-        return ghosts[at : at + PATCH_DEV, :]
+        return ghosts_ref[at : at + PATCH_DEV, :]
 
     def beside(c, side):
         st = state[c]
         g = ghost(side, c)
+        found = found_ref[side, :PATCH_DEV, :1] > 0.5
         if side == 0:
             wide = jnp.concatenate([pltpu.roll(g, FP, 1)] * groups, axis=1)
             edge, moved = lane < FP, pltpu.roll(st, FP, 1)
@@ -408,7 +437,7 @@
         else:
             wide = jnp.concatenate([pltpu.roll(g, 63 - k, 1) for k in range(groups)], axis=1)
             edge, moved = col == FP - 1, pltpu.roll(st, FP * FP - 1, 1)
-        return jnp.where(edge, jnp.where(founds[side], wide, st), moved)
+        return jnp.where(edge, jnp.where(found, wide, st), moved)
 
     sides = [[beside(c, side) for c in range(3)] for side in range(4)]
 
@@ -431,19 +460,7 @@
         if c == 0:
             updated = updated + uplift_rate * lift
         wout_ref[c] = updated
-
-    store_a.wait()
-    store_b.wait()
-    for has_target, _, copy in halos:
-        pl.when(has_target)(copy.wait_send)
-    pltpu.make_async_copy(some, some, st_send).wait()
-    for i in range(1, ngz):
-        hand(i).wait_send()
-
-    @pl.when(gz == 0)
-    def _():
-        sent = slots.at[pl.ds(0, ndev - 1)]
-        pltpu.make_async_copy(sent, sent, lift_send).wait()
+    store.wait()
 
 
 def per_device(volume, materials, water_height, water_flow, owner_of, patch_tile):
@@ -455,20 +472,23 @@
     f32 = jnp.float32
     dma = pltpu.SemaphoreType.DMA
     vmem = pl.BlockSpec(memory_space=pltpu.VMEM)
-    anywhere = pl.BlockSpec(memory_space=pl.ANY)
-    return pl.pallas_call(
+    hbm = pl.BlockSpec(memory_space=pltpu.HBM)
+    whole = functools.partial(pltpu.with_memory_space_constraint, memory_space=pltpu.VMEM)
+    middle = pl.pallas_call(
         functools.partial(kernel, (ngx, ngy, ngz, patches, depth, cx)),
         name="coupled_step",
         out_shape=(
-            jax.ShapeDtypeStruct(volume.shape, f32),
-            jax.ShapeDtypeStruct((3,) + water_height.shape, f32),
+            pltpu.VMEM(volume.shape, f32),
+            pltpu.VMEM((3,) + water_height.shape, f32),
+            pltpu.VMEM((96, LANES), f32),
+            pltpu.VMEM((4, 8, LANES), f32),
+            pltpu.VMEM((2, 8, LANES), f32),
         ),
-        in_specs=[vmem, vmem, vmem, vmem, anywhere, anywhere],
-        out_specs=(anywhere, vmem),
+        in_specs=[hbm] * 6,
+        out_specs=(vmem,) * 5,
         scratch_shapes=[
             pltpu.VMEM((fields, depth + 2, cx + 16, LANES), f32),
             pltpu.VMEM(materials.shape, f32),
-            pltpu.VMEM(volume.shape, f32),
             pltpu.VMEM((cx, LANES), f32),
             pltpu.VMEM((cx, LANES), f32),
             pltpu.VMEM((cx, LANES), f32),
@@ -476,14 +496,30 @@
             pltpu.VMEM((ngz, nblk, 24, LANES), f32),
             pltpu.VMEM((ndev, 2, LANES), f32),
             pltpu.VMEM((nblk, 2, LANES), f32),
-            dma, dma, dma((2,)), dma((6,)), dma((6,)), dma, dma,
+            pltpu.VMEM((1, patches), jnp.int32), pltpu.VMEM((1, patches), jnp.int32),
+            dma, dma, dma((4,)), dma((6,)), dma((6,)), dma, dma,
             dma((max(ngz - 1, 1),)), dma((max(ngz - 1, 1),)), dma, dma,
         ],
-        compiler_params=pltpu.CompilerParams(collective_id=0, has_side_effects=True, vmem_limit_bytes=56 * 1024 * 1024),
+        compiler_params=pltpu.CompilerParams(
+            collective_id=0, has_side_effects=True, vmem_limit_bytes=40 * 1024 * 1024
+        ),
     )(
         owner_of.reshape(1, patches), patch_tile.reshape(1, patches),
         water_height, water_flow, volume, materials,
     )
+    middle = [whole(part) for part in middle]
+    return pl.pallas_call(
+        finish,
+        name="finish_step",
+        out_shape=(
+            jax.ShapeDtypeStruct(volume.shape, f32),
+            jax.ShapeDtypeStruct((3,) + water_height.shape, f32),
+        ),
+        in_specs=[vmem] * 5,
+        out_specs=(hbm, vmem),
+        scratch_shapes=[dma],
+        compiler_params=pltpu.CompilerParams(vmem_limit_bytes=16 * 1024 * 1024),
+    )(*middle)
 
 
 def solution(mesh):

time: 24.6 us -> 26.9 us (1.093)
  local copies, waits for them, and re-layouts: 4.08 us -> 5.84 us
  Pallas kernels: 19.7 us -> 20.1 us
    pallas_call x0 -> x1, Pallas kernels: none -> 2.7 us  [per_device(): pl.pallas_call(finish, name='finish_step', out_shape=(jax.ShapeDtypeStruc...]
    pallas_call x1, Pallas kernels: 19.7 us -> 17.4 us  [per_device(): pl.pallas_call(functools.partial(kernel, (ngx, ngy, ngz, patches, depth,...]
    unnamed x4 -> x12, local copies, waits for them, and re-layouts: 4.08 us -> 5.84 us
where the time goes in v1:
time: 26.9 us; the launch traced here: 26.6 us
  Pallas kernels  20.1 us (75%)
  local copies, waits for them, and re-layouts  5.84 us (22%)
  between operations  0.65 us (2%)
    pallas_call x1, Pallas kernels, per_device(): pl.pallas_call(functools.partial(kernel, (ngx, ngy, ngz, patches, depth,...  17.4 us
    unnamed x12, local copies, waits for them, and re-layouts  5.84 us
    pallas_call x1, Pallas kernels, per_device(): pl.pallas_call(finish, name='finish_step', out_shape=(jax.ShapeDtypeStruc...  2.7 us

profile of v1, /device:TPU:0, one launch (start us, length us, event | category | flops | bytes accessed | tf_op | source)
XLA Modules:
  0.0 26.6 jit_solution(6467791305490190803)
XLA Ops:
  0.6 0.0 copy-start
  0.6 1.7 %copy-done = f32[9,8,64,128]{3,2,1,0:T(8,128)S(1)} copy-done((f32[9,8,64,128]{3,2,1,0:T(8,128)S(1)}, f32[9,8,64,128]{3,2,1,0:T(8,128)}, u32[]{:S(2)}) %copy-start) | copy-done | bytes 2359320
  2.3 0.0 copy-start.1
  2.3 1.1 %copy-done.1 = f32[3,8,64,128]{3,2,1,0:T(8,128)S(1)} copy-done((f32[3,8,64,128]{3,2,1,0:T(8,128)S(1)}, f32[3,8,64,128]{3,2,1,0:T(8,128)}, u32[]{:S(2)}) %copy-start.1) | copy-done | bytes 786456
  3.4 0.0 copy-start.2
  3.4 0.9 %copy-done.2 = f32[2,4,4096]{2,1,0:T(4,128)S(1)} copy-done((f32[2,4,4096]{2,1,0:T(4,128)S(1)}, f32[2,4,4096]{2,1,0:T(4,128)}, u32[]{:S(2)}) %copy-start.2) | copy-done | bytes 131096
  4.3 0.0 copy-start.3
  4.3 0.8 %copy-done.3 = f32[4,4096]{1,0:T(4,128)S(1)} copy-done((f32[4,4096]{1,0:T(4,128)S(1)}, f32[4,4096]{1,0:T(4,128)}, u32[]{:S(2)}) %copy-start.3) | copy-done | bytes 65560
  5.2 0.0 copy-start.4
  5.2 0.7 %copy-done.4 = s32[128]{0:T(128)S(1)} copy-done((s32[128]{0:T(128)S(1)}, s32[128]{0:T(128)}, u32[]{:S(2)}) %copy-start.4) | copy-done | bytes 536
  5.8 0.0 copy-start.5
  5.8 0.7 %copy-done.5 = s32[128]{0:T(128)S(1)} copy-done((s32[128]{0:T(128)S(1)}, s32[128]{0:T(128)}, u32[]{:S(2)}) %copy-start.5) | copy-done | bytes 536
  6.5 17.4 %coupled_step.1 = (f32[9,8,64,128]{3,2,1,0:T(8,128)S(1)}, f32[3,4,4096]{2,1,0:T(4,128)S(1)}, f32[96,128]{1,0:T(8,128)S(1)}, f32[4,8,128]{2,1,0:T(8,128)S(1)}, f32[2,8,128]{2,1,0:T(8,128)S(1)}) custom-call(s32[1,128]{1,0:T(1,128)S(1)} %bitcast.2, s32[1,128]{1,0:T(1,128)S(1)} %bitcast.3, f32[4,4096]{1,0:T(4,128)S(1)} %copy-done.3, ...), custom_call_target="tpu_custom_call" | custom-call | tf_op jit(solution)/shard_map/coupled_step/pallas_call | solution.py:477
  23.9 2.7 %finish_step.1 = (f32[9,8,64,128]{3,2,1,0:T(8,128)}, f32[3,4,4096]{2,1,0:T(4,128)}) custom-call(f32[9,8,64,128]{3,2,1,0:T(8,128)S(1)} %get-tuple-element.7.outv, f32[3,4,4096]{2,1,0:T(4,128)S(1)} %get-tuple-element.8.state_ref, f32[96,128]{1,0:T(8,128)S(1)} %get-tuple-element.9.ghosts_ref, f32[4,8,128]{2,1,0:T(8,128)S(1)} %get-tuple-element.10.found_ref, ...), custom_call_target="tpu_custom_call" | custom-call | tf_op jit(solution)/shard_map/finish_step/pallas_call | solution.py:511
Async XLA Ops:
  0.6 1.7 %copy-start = (f32[9,8,64,128]{3,2,1,0:T(8,128)S(1)}, f32[9,8,64,128]{3,2,1,0:T(8,128)}, u32[]{:S(2)}) copy-start(f32[9,8,64,128]{3,2,1,0:T(8,128)} %vol_hbm.1) | copy-start | bytes 7077892
  2.3 1.1 %copy-start.1 = (f32[3,8,64,128]{3,2,1,0:T(8,128)S(1)}, f32[3,8,64,128]{3,2,1,0:T(8,128)}, u32[]{:S(2)}) copy-start(f32[3,8,64,128]{3,2,1,0:T(8,128)} %mat_hbm.1) | copy-start | bytes 2359300
  3.4 0.9 %copy-start.2 = (f32[2,4,4096]{2,1,0:T(4,128)S(1)}, f32[2,4,4096]{2,1,0:T(4,128)}, u32[]{:S(2)}) copy-start(f32[2,4,4096]{2,1,0:T(4,128)} %fl_hbm.1) | copy-start | bytes 393220
  4.3 0.8 %copy-start.3 = (f32[4,4096]{1,0:T(4,128)S(1)}, f32[4,4096]{1,0:T(4,128)}, u32[]{:S(2)}) copy-start(f32[4,4096]{1,0:T(4,128)} %h_hbm.1) | copy-start | bytes 196612
  5.2 0.7 %copy-start.4 = (s32[128]{0:T(128)S(1)}, s32[128]{0:T(128)}, u32[]{:S(2)}) copy-start(s32[128]{0:T(128)} %param.10) | copy-start | bytes 1540
  5.8 0.7 %copy-start.5 = (s32[128]{0:T(128)S(1)}, s32[128]{0:T(128)}, u32[]{:S(2)}) copy-start(s32[128]{0:T(128)} %param.11) | copy-start | bytes 1540

commit v2 on v1

--- a/solution.py
+++ b/solution.py
@@ -504,8 +504,13 @@
             collective_id=0, has_side_effects=True, vmem_limit_bytes=40 * 1024 * 1024
         ),
     )(
-        owner_of.reshape(1, patches), patch_tile.reshape(1, patches),
-        water_height, water_flow, volume, materials,
+        *[
+            pltpu.with_memory_space_constraint(part, pltpu.HBM)
+            for part in (
+                owner_of.reshape(1, patches), patch_tile.reshape(1, patches),
+                water_height, water_flow, volume, materials,
+            )
+        ]
     )
     middle = [whole(part) for part in middle]
     return pl.pallas_call(

time: 26.9 us -> 20.5 us (0.76)
  local copies, waits for them, and re-layouts: 5.84 us -> 0 us
  Pallas kernels: 20.1 us -> 19.7 us
    unnamed x12 -> x0, local copies, waits for them, and re-layouts: 5.84 us -> none
    pallas_call x1, Pallas kernels: 17.4 us -> 17 us  [per_device(): pl.pallas_call(functools.partial(kernel, (ngx, ngy, ngz, patches, depth,...]
where the time goes in v2:
time: 20.5 us; the launch traced here: 20.3 us
  Pallas kernels  19.7 us (96%)
  between operations  0.64 us (3%)
    pallas_call x1, Pallas kernels, per_device(): pl.pallas_call(functools.partial(kernel, (ngx, ngy, ngz, patches, depth,...  17 us
    pallas_call x1, Pallas kernels, per_device(): pl.pallas_call(finish, name='finish_step', out_shape=(jax.ShapeDtypeStruc...  2.68 us

profile of v2, /device:TPU:0, one launch (start us, length us, event | category | flops | bytes accessed | tf_op | source)
XLA Modules:
  0.0 20.3 jit_solution(14729857741685568657)
XLA Ops:
  0.6 17.0 %coupled_step.1 = (f32[9,8,64,128]{3,2,1,0:T(8,128)S(1)}, f32[3,4,4096]{2,1,0:T(4,128)S(1)}, f32[96,128]{1,0:T(8,128)S(1)}, f32[4,8,128]{2,1,0:T(8,128)S(1)}, f32[2,8,128]{2,1,0:T(8,128)S(1)}) custom-call(s32[1,128]{1,0:T(1,128)} %bitcast.2, s32[1,128]{1,0:T(1,128)} %bitcast.3, f32[4,4096]{1,0:T(4,128)} %h_hbm.1, f32[2,4,4096]{2,1,0:T(4,128)} %fl_hbm.1, ...), custom_call_target="tpu_custom_call" | custom-call | tf_op jit(solution)/shard_map/coupled_step/pallas_call | solution.py:477
  17.6 2.7 %finish_step.1 = (f32[9,8,64,128]{3,2,1,0:T(8,128)}, f32[3,4,4096]{2,1,0:T(4,128)}) custom-call(f32[9,8,64,128]{3,2,1,0:T(8,128)S(1)} %get-tuple-element.7.outv, f32[3,4,4096]{2,1,0:T(4,128)S(1)} %get-tuple-element.8.state_ref, f32[96,128]{1,0:T(8,128)S(1)} %get-tuple-element.9.ghosts_ref, f32[4,8,128]{2,1,0:T(8,128)S(1)} %get-tuple-element.10.found_ref, ...), custom_call_target="tpu_custom_call" | custom-call | tf_op jit(solution)/shard_map/finish_step/pallas_call | solution.py:516

commit v3 on v2

--- a/solution.py
+++ b/solution.py
@@ -67,11 +67,24 @@
     return (six[0] + six[1] + six[2] + six[3] + six[4] + six[5]) * (1.0 / 6.0)
 
 
+def neighbour_terms(part):
+    height, flow_x, flow_y = part
+    speed_x, speed_y = flow_x / height, flow_y / height
+    head = 0.5 * gravity * height * height
+    flux_x = [flow_x, flow_x * speed_x + head, flow_y * speed_x]
+    flux_y = [flow_y, flow_x * speed_y, flow_y * speed_y + head]
+    return [
+        [0.25 * u + sign * flux_ratio * f for u, f in zip(part, flux)]
+        for flux in (flux_x, flux_y)
+        for sign in (1.0, -1.0)
+    ]
+
+
 def kernel(
     sizes,
     own_hbm, til_hbm, h_hbm, fl_hbm, vol_hbm, mat_hbm,
-    outv, state_out, ghosts_out, found_out, coarse_out,
-    ext, mat, ys_lo, ys_hi, yl, yr, strips, slots, lifts,
+    outv, base_out, delta_out, coarse_out,
+    state_in, ext, mat, ys_lo, ys_hi, yl, yr, strips, slots, lifts,
     own_ref, til_ref, vol_sem, mat_sem, in_sem, halo_send, halo_recv, st_send, st_recv, sib_send, sib_recv,
     lift_send, lift_recv,
 ):
@@ -91,8 +104,8 @@
         vol_hbm, ext.at[:, pl.ds(1, depth), pl.ds(8, cx), :], vol_sem
     )
     ins = [
-        pltpu.make_async_copy(h_hbm, state_out.at[0], in_sem.at[0]),
-        pltpu.make_async_copy(fl_hbm, state_out.at[pl.ds(1, 2)], in_sem.at[1]),
+        pltpu.make_async_copy(h_hbm, state_in.at[0], in_sem.at[0]),
+        pltpu.make_async_copy(fl_hbm, state_in.at[pl.ds(1, 2)], in_sem.at[1]),
         pltpu.make_async_copy(own_hbm, own_ref, in_sem.at[2]),
         pltpu.make_async_copy(til_hbm, til_ref, in_sem.at[3]),
     ]
@@ -140,20 +153,38 @@
     half = lane4 & (FP - 1)
     for copy in ins:
         copy.wait()
-    state = [state_out[0], state_out[1], state_out[2]]
+    state = [state_in[0], state_in[1], state_in[2]]
     groups = FP * FP // LANES
+    rows_own, cols_own = [], []
     for c in range(3):
         st = state[c]
-        strips[gz, blk, 4 * c : 4 * c + 4, :] = jnp.where(
-            lane4 < FP, st[:, :LANES], st[:, FP * FP - LANES :]
-        )
+        rows_own.append(jnp.where(lane4 < FP, st[:, :LANES], st[:, FP * FP - LANES :]))
+        strips[gz, blk, 4 * c : 4 * c + 4, :] = rows_own[c]
         packed = jnp.zeros((PATCH_DEV, LANES), jnp.float32)
         for k in range(groups):
             part = st[:, LANES * k : LANES * (k + 1)]
             first = part if k == 0 else pltpu.roll(part, k, 1)
             packed = jnp.where(half == k, first, packed)
             packed = jnp.where(half == 32 + k, pltpu.roll(part, (k + 97) % LANES, 1), packed)
+        cols_own.append(packed)
         strips[gz, blk, 12 + 4 * c : 16 + 4 * c, :] = packed
+
+    lane_w = iota((PATCH_DEV, FP * FP), 1)
+    col_w = lane_w & (FP - 1)
+    span = FP * FP
+    terms = neighbour_terms(state)
+    moves = [
+        (lane_w < FP, FP),
+        (lane_w >= span - FP, span - FP),
+        (col_w == 0, 1),
+        (col_w == FP - 1, span - 1),
+    ]
+    for c in range(3):
+        moved = [
+            jnp.where(edge, terms[side][c], pltpu.roll(terms[side][c], shift, 1))
+            for side, (edge, shift) in enumerate(moves)
+        ]
+        base_out[c] = (moved[0] + moved[1]) + (moved[2] + moved[3])
 
     vol_copy.wait()
 
@@ -232,7 +263,7 @@
     my_y = my_tile & (tiles_y - 1)
     my_blk = (my_x >> log2(local_x)) * ngy + (my_y >> log2(local_y))
 
-    picks = []
+    founds, picks = [], []
     keys = (8, ndev * 24)
     for side, (valid, want) in enumerate(
         [
@@ -244,7 +275,7 @@
     ):
         match = tile8 == jnp.where(valid, want, -1)
         other = pick_sum(match, row_of8 + 1) - 1
-        found_out[side] = jnp.broadcast_to(jnp.where(other >= 0, 1.0, 0.0), (8, LANES))
+        founds.append((other >= 0)[:PATCH_DEV])
         dev = other >> log2(PATCH_DEV)
         place = (dev & (ngz - 1)) * nblk + (dev >> log2(ngz))
         target = place * 24 + (other & (PATCH_DEV - 1))
@@ -369,7 +400,25 @@
 
     for i in range(1, ngz):
         hand(i).wait_recv()
-    ghosts_out[...] = exact_dot(pick_all, strips[...].reshape(ndev * 24, LANES))
+    ghosts = exact_dot(pick_all, strips[...].reshape(ndev * 24, LANES))
+
+    changes = []
+    for side, (own, shift) in enumerate(
+        [(rows_own, FP), (rows_own, FP), (cols_own, 96), (cols_own, 32)]
+    ):
+        part = [
+            jnp.where(
+                founds[side],
+                pltpu.roll(ghosts[at : at + PATCH_DEV, :], shift, 1),
+                own[c],
+            )
+            for c, at in enumerate(range(side * 24, side * 24 + 24, 8))
+        ]
+        new, old = neighbour_terms(part)[side], neighbour_terms(own)[side]
+        changes.append([new[c] - old[c] for c in range(3)])
+    for c in range(3):
+        delta_out[c, :PATCH_DEV, :] = jnp.where(lane4 < FP, changes[0][c], changes[1][c])
+        delta_out[3 + c, :PATCH_DEV, :] = jnp.where(half < 32, changes[2][c], changes[3][c])
 
     @pl.when(gz == 0)
     def _():
@@ -381,7 +430,7 @@
         pltpu.make_async_copy(lifts, lifts, lift_recv).wait()
 
     for k in range(2):
-        coarse_out[k] = exact_dot(chooser, lifts[:, k, :])
+        coarse_out[8 * k : 8 * k + 8, :] = exact_dot(chooser, lifts[:, k, :])
 
     for has_target, _, copy in halos:
         pl.when(has_target)(copy.wait_send)
@@ -395,71 +444,35 @@
         pltpu.make_async_copy(sent, sent, lift_send).wait()
 
 
-def finish(
-    outv, state_ref, ghosts_ref, found_ref, coarse_ref, vout_hbm, wout_ref, out_sem
-):
+def finish(outv, base_ref, delta_ref, coarse_ref, vout_hbm, wout_ref, out_sem):
     store = pltpu.make_async_copy(outv, vout_hbm, out_sem)
     store.start()
-    state = [state_ref[0], state_ref[1], state_ref[2]]
     groups = FP * FP // LANES
     wide_lane = iota((LANES, 8 * LANES), 1)
     source = (wide_lane >> log2(LANES)) * PS + ((wide_lane & (FP - 1)) >> log2(REFINE))
     expand = jnp.where(iota((LANES, 8 * LANES), 0) == source, 1.0, 0.0)
-    fine = [exact_dot(coarse_ref[k], expand)[:PATCH_DEV] for k in range(2)]
-    lift = jnp.concatenate(
-        [
-            fine[(k // 2) // 8][:, LANES * ((k // 2) % 8) : LANES * ((k // 2) % 8 + 1)]
-            for k in range(groups)
-        ],
-        axis=1,
-    )
-
-    lane = iota((PATCH_DEV, FP * FP), 1)
-    col = lane & (FP - 1)
-
-    def ghost(side, c):
-        at = (side * 3 + c) * 8
-        return ghosts_ref[at : at + PATCH_DEV, :]
-
-    def beside(c, side):
-        st = state[c]
-        g = ghost(side, c)
-        found = found_ref[side, :PATCH_DEV, :1] > 0.5
-        if side == 0:
-            wide = jnp.concatenate([pltpu.roll(g, FP, 1)] * groups, axis=1)
-            edge, moved = lane < FP, pltpu.roll(st, FP, 1)
-        elif side == 1:
-            wide = jnp.concatenate([pltpu.roll(g, FP, 1)] * groups, axis=1)
-            edge, moved = lane >= FP * FP - FP, pltpu.roll(st, FP * FP - FP, 1)
-        elif side == 2:
-            wide = jnp.concatenate([pltpu.roll(g, 96 - k, 1) for k in range(groups)], axis=1)
-            edge, moved = col == 0, pltpu.roll(st, 1, 1)
-        else:
-            wide = jnp.concatenate([pltpu.roll(g, 63 - k, 1) for k in range(groups)], axis=1)
-            edge, moved = col == FP - 1, pltpu.roll(st, FP * FP - 1, 1)
-        return jnp.where(edge, jnp.where(found, wide, st), moved)
-
-    sides = [[beside(c, side) for c in range(3)] for side in range(4)]
-
-    def fluxes_x(part):
-        height, flow_x, flow_y = part
-        speed = flow_x / height
-        return [flow_x, flow_x * speed + 0.5 * gravity * height * height, flow_y * speed]
-
-    def fluxes_y(part):
-        height, flow_x, flow_y = part
-        speed = flow_y / height
-        return [flow_y, flow_x * speed, flow_y * speed + 0.5 * gravity * height * height]
-
-    fw, fe = fluxes_x(sides[0]), fluxes_x(sides[1])
-    fs, fn = fluxes_y(sides[2]), fluxes_y(sides[3])
+    fine = exact_dot(coarse_ref[...], expand)
+    lane4 = iota((PATCH_DEV, LANES), 1)
+    half = lane4 & (FP - 1)
     for c in range(3):
-        updated = 0.25 * (sides[1][c] + sides[0][c] + sides[3][c] + sides[2][c]) - flux_ratio * (
-            (fe[c] - fw[c]) + (fn[c] - fs[c])
-        )
-        if c == 0:
-            updated = updated + uplift_rate * lift
-        wout_ref[c] = updated
+        rows = delta_ref[c, :PATCH_DEV, :]
+        cols = delta_ref[3 + c, :PATCH_DEV, :]
+        for k in range(groups):
+            at = pl.ds(LANES * k, LANES)
+            value = base_ref[c, :, at]
+            low = cols if k == 0 else pltpu.roll(cols, LANES - k, 1)
+            high = cols if k == 31 else pltpu.roll(cols, (31 - k) % LANES, 1)
+            value = value + jnp.where(half == 0, low, jnp.where(half == FP - 1, high, 0.0))
+            if k == 0:
+                value = value + jnp.where(lane4 < FP, rows, 0.0)
+            if k == groups - 1:
+                value = value + jnp.where(lane4 < FP, 0.0, rows)
+            if c == 0:
+                r = k // 2
+                top = 8 * (r // 8)
+                lift = fine[top : top + PATCH_DEV, LANES * (r % 8) : LANES * (r % 8 + 1)]
+                value = value + uplift_rate * lift
+            wout_ref[c, :, at] = value
     store.wait()
 
 
@@ -480,13 +493,13 @@
         out_shape=(
             pltpu.VMEM(volume.shape, f32),
             pltpu.VMEM((3,) + water_height.shape, f32),
-            pltpu.VMEM((96, LANES), f32),
-            pltpu.VMEM((4, 8, LANES), f32),
-            pltpu.VMEM((2, 8, LANES), f32),
+            pltpu.VMEM((6, 8, LANES), f32),
+            pltpu.VMEM((16, LANES), f32),
         ),
         in_specs=[hbm] * 6,
-        out_specs=(vmem,) * 5,
+        out_specs=(vmem,) * 4,
         scratch_shapes=[
+            pltpu.VMEM((3,) + water_height.shape, f32),
             pltpu.VMEM((fields, depth + 2, cx + 16, LANES), f32),
             pltpu.VMEM(materials.shape, f32),
             pltpu.VMEM((cx, LANES), f32),
@@ -520,7 +533,7 @@
             jax.ShapeDtypeStruct(volume.shape, f32),
             jax.ShapeDtypeStruct((3,) + water_height.shape, f32),
         ),
-        in_specs=[vmem] * 5,
+        in_specs=[vmem] * 4,
         out_specs=(hbm, vmem),
         scratch_shapes=[dma],
         compiler_params=pltpu.CompilerParams(vmem_limit_bytes=16 * 1024 * 1024),

time: 20.5 us -> 20.2 us (0.985)
  Pallas kernels: 19.7 us -> 19.4 us
    pallas_call x1, Pallas kernels: 2.68 us -> 2.39 us  [per_device(): pl.pallas_call(finish, name='finish_step', out_shape=(jax.ShapeDtypeStruc...]
where the time goes in v3:
time: 20.2 us; the launch traced here: 20 us
  Pallas kernels  19.4 us (96%)
  between operations  0.64 us (3%)
    pallas_call x1, Pallas kernels, per_device(): pl.pallas_call(functools.partial(kernel, (ngx, ngy, ngz, patches, depth,...  17 us
    pallas_call x1, Pallas kernels, per_device(): pl.pallas_call(finish, name='finish_step', out_shape=(jax.ShapeDtypeStruc...  2.39 us

profile of v3, /device:TPU:0, one launch (start us, length us, event | category | flops | bytes accessed | tf_op | source)
XLA Modules:
  0.0 20.0 jit_solution(14831184364656583424)
XLA Ops:
  0.6 17.0 %coupled_step.1 = (f32[9,8,64,128]{3,2,1,0:T(8,128)S(1)}, f32[3,4,4096]{2,1,0:T(4,128)S(1)}, f32[6,8,128]{2,1,0:T(8,128)S(1)}, f32[16,128]{1,0:T(8,128)S(1)}) custom-call(s32[1,128]{1,0:T(1,128)} %bitcast.2, s32[1,128]{1,0:T(1,128)} %bitcast.3, f32[4,4096]{1,0:T(4,128)} %h_hbm.1, f32[2,4,4096]{2,1,0:T(4,128)} %fl_hbm.1, f32[9,8,64,128]{3,2,1,0:T(8,128)} %vol_hbm.1, ...), custom_call_target="tpu_custom_call" | custom-call | tf_op jit(solution)/shard_map/coupled_step/pallas_call | solution.py:490
  17.6 2.4 %finish_step.1 = (f32[9,8,64,128]{3,2,1,0:T(8,128)}, f32[3,4,4096]{2,1,0:T(4,128)}) custom-call(f32[9,8,64,128]{3,2,1,0:T(8,128)S(1)} %get-tuple-element.6.outv, f32[3,4,4096]{2,1,0:T(4,128)S(1)} %get-tuple-element.7.base_ref, f32[6,8,128]{2,1,0:T(8,128)S(1)} %get-tuple-element.8.delta_ref, f32[16,128]{1,0:T(8,128)S(1)} %get-tuple-element.9.coarse_ref), custom_call_target="tpu_custom_call" | custom-call | tf_op jit(solution)/shard_map/finish_step/pallas_call | solution.py:529

commit v4 on v3

--- a/solution.py
+++ b/solution.py
@@ -100,9 +100,12 @@
     def coords(d):
         return (d // (ngy * ngz), (d // ngz) % ngy, d % ngz)
 
-    vol_copy = pltpu.make_async_copy(
-        vol_hbm, ext.at[:, pl.ds(1, depth), pl.ds(8, cx), :], vol_sem
-    )
+    vol_copies = [
+        pltpu.make_async_copy(
+            vol_hbm.at[f], ext.at[f, pl.ds(1, depth), pl.ds(8, cx), :], vol_sem.at[f]
+        )
+        for f in range(9)
+    ]
     ins = [
         pltpu.make_async_copy(h_hbm, state_in.at[0], in_sem.at[0]),
         pltpu.make_async_copy(fl_hbm, state_in.at[pl.ds(1, 2)], in_sem.at[1]),
@@ -111,7 +114,8 @@
     ]
     for copy in ins:
         copy.start()
-    vol_copy.start()
+    for copy in vol_copies:
+        copy.start()
     mat_copy = pltpu.make_async_copy(mat_hbm, mat, mat_sem)
     mat_copy.start()
 
@@ -186,7 +190,8 @@
         ]
         base_out[c] = (moved[0] + moved[1]) + (moved[2] + moved[3])
 
-    vol_copy.wait()
+    for copy in vol_copies:
+        copy.wait()
 
     lane_c = iota((cx, LANES), 1)
 
@@ -445,8 +450,11 @@
 
 
 def finish(outv, base_ref, delta_ref, coarse_ref, vout_hbm, wout_ref, out_sem):
-    store = pltpu.make_async_copy(outv, vout_hbm, out_sem)
-    store.start()
+    stores = [
+        pltpu.make_async_copy(outv.at[f], vout_hbm.at[f], out_sem.at[f]) for f in range(9)
+    ]
+    for store in stores:
+        store.start()
     groups = FP * FP // LANES
     wide_lane = iota((LANES, 8 * LANES), 1)
     source = (wide_lane >> log2(LANES)) * PS + ((wide_lane & (FP - 1)) >> log2(REFINE))
@@ -473,7 +481,8 @@
                 lift = fine[top : top + PATCH_DEV, LANES * (r % 8) : LANES * (r % 8 + 1)]
                 value = value + uplift_rate * lift
             wout_ref[c, :, at] = value
-    store.wait()
+    for store in stores:
+        store.wait()
 
 
 def per_device(volume, materials, water_height, water_flow, owner_of, patch_tile):
@@ -510,7 +519,7 @@
             pltpu.VMEM((ndev, 2, LANES), f32),
             pltpu.VMEM((nblk, 2, LANES), f32),
             pltpu.VMEM((1, patches), jnp.int32), pltpu.VMEM((1, patches), jnp.int32),
-            dma, dma, dma((4,)), dma((6,)), dma((6,)), dma, dma,
+            dma((fields,)), dma, dma((4,)), dma((6,)), dma((6,)), dma, dma,
             dma((max(ngz - 1, 1),)), dma((max(ngz - 1, 1),)), dma, dma,
         ],
         compiler_params=pltpu.CompilerParams(
@@ -535,7 +544,7 @@
         ),
         in_specs=[vmem] * 4,
         out_specs=(hbm, vmem),
-        scratch_shapes=[dma],
+        scratch_shapes=[dma((fields,))],
         compiler_params=pltpu.CompilerParams(vmem_limit_bytes=16 * 1024 * 1024),
     )(*middle)
 

time: 20.2 us -> 20.5 us (1.015)
  Pallas kernels: 19.4 us -> 19.7 us
    pallas_call x1, Pallas kernels: 17 us -> 17.2 us  [per_device(): pl.pallas_call(functools.partial(kernel, (ngx, ngy, ngz, patches, depth,...]
where the time goes in v4:
time: 20.5 us; the launch traced here: 20.3 us
  Pallas kernels  19.7 us (96%)
  between operations  0.64 us (3%)
    pallas_call x1, Pallas kernels, per_device(): pl.pallas_call(functools.partial(kernel, (ngx, ngy, ngz, patches, depth,...  17.2 us
    pallas_call x1, Pallas kernels, per_device(): pl.pallas_call(finish, name='finish_step', out_shape=(jax.ShapeDtypeStruc...  2.44 us

profile of v4, /device:TPU:0, one launch (start us, length us, event | category | flops | bytes accessed | tf_op | source)
XLA Modules:
  0.0 20.3 jit_solution(3904277453438187324)
XLA Ops:
  0.6 17.2 %coupled_step.1 = (f32[9,8,64,128]{3,2,1,0:T(8,128)S(1)}, f32[3,4,4096]{2,1,0:T(4,128)S(1)}, f32[6,8,128]{2,1,0:T(8,128)S(1)}, f32[16,128]{1,0:T(8,128)S(1)}) custom-call(s32[1,128]{1,0:T(1,128)} %bitcast.2, s32[1,128]{1,0:T(1,128)} %bitcast.3, f32[4,4096]{1,0:T(4,128)} %h_hbm.1, f32[2,4,4096]{2,1,0:T(4,128)} %fl_hbm.1, f32[9,8,64,128]{3,2,1,0:T(8,128)} %vol_hbm.1, ...), custom_call_target="tpu_custom_call" | custom-call | tf_op jit(solution)/shard_map/coupled_step/pallas_call | solution.py:499
  17.9 2.4 %finish_step.1 = (f32[9,8,64,128]{3,2,1,0:T(8,128)}, f32[3,4,4096]{2,1,0:T(4,128)}) custom-call(f32[9,8,64,128]{3,2,1,0:T(8,128)S(1)} %get-tuple-element.6.outv, f32[3,4,4096]{2,1,0:T(4,128)S(1)} %get-tuple-element.7.base_ref, f32[6,8,128]{2,1,0:T(8,128)S(1)} %get-tuple-element.8.delta_ref, f32[16,128]{1,0:T(8,128)S(1)} %get-tuple-element.9.coarse_ref), custom_call_target="tpu_custom_call" | custom-call | tf_op jit(solution)/shard_map/finish_step/pallas_call | solution.py:538
